TPU v7x, 32 devices: a whole 2x2x4 slice. The times are simulated.
32 devices in a mesh: shard: 16 (over z, x, core), replica: 2 (over y).
Axes of the slice: x: 2, y: 2, z: 4, core: 2. Of those that a mesh axis runs over, the one named last changes fastest.
Arguments:
- x_in: bfloat16 [2, 8192, 768], P('replica', 'shard'), may hold values from -6 to 6
- seq_units: int32 [2, 16], P('replica'), may hold values from 1 to 64, 512 in all within a row
- deal: int32 [2, 16], P('replica'), may hold values from 0 to 15, each once within a row
- gain_attn: float32 [768], replicated, may hold values from 0.1 to 1.9
- w_query: bfloat16 [768, 768], P('shard'), may hold values from -0.4375 to 0.4375
- w_key: bfloat16 [768, 768], P('shard'), may hold values from -0.21875 to 0.21875
- w_value: bfloat16 [768, 768], P('shard'), may hold values from -0.21875 to 0.21875
- w_out: bfloat16 [768, 768], P('shard'), may hold values from -0.875 to 0.875
- gain_ffn: float32 [768], replicated, may hold values from 0.1 to 1.9
- w_gate: bfloat16 [768, 2048], P('shard'), may hold values from -0.21875 to 0.21875
- w_up: bfloat16 [768, 2048], P('shard'), may hold values from -0.21875 to 0.21875
- w_down: bfloat16 [2048, 768], P('shard'), may hold values from -0.125 to 0.125
- d_out: bfloat16 [2, 16, 1024, 768], P('replica', 'shard'), may hold values from -6 to 6
Outputs:
- layer_out: bfloat16 [2, 16, 1024, 768], P('replica', 'shard')
- grad_x: bfloat16 [2, 8192, 768], P('replica', 'shard')
- grad_gain_attn: float32 [768], P('shard')
- grad_gain_ffn: float32 [768], P('shard')
- grad_w_query: float32 [768, 768], P('shard')
- grad_w_key: float32 [768, 768], P('shard')
- grad_w_value: float32 [768, 768], P('shard')
- grad_w_out: float32 [768, 768], P('shard')
- grad_w_gate: float32 [768, 2048], P('shard')
- grad_w_up: float32 [768, 2048], P('shard')
- grad_w_down: float32 [2048, 768], P('shard')
Inputs may be any that keep to these rules, and one draw needn't show every extreme that they name: `seq_units`: each group's 16 entries sum to 512. `deal`: each group's row names every sequence 0 to 15 once.
All inputs are finite; a program needn't handle non-finite values.
Results may differ from a plain program's by a relative error of at most 0.023.
Values may be sent and summed in bfloat16 or wider, within the bound.
No kernel may reach another device: no remote copies, remote signals or barrier semaphores. Data moves between devices by JAX's collectives and lax.ppermute only.
A program may use at most 320 MiB of HBM per device.

v0:
```python
import jax
import jax.numpy as jnp
from jax import lax
from jax.sharding import PartitionSpec as P

H = 12
HD = 64
norm_eps = 1e-06
neg_big = -1e30


def rms_scale(tok_rows, gain_vec):
    inverse = lax.rsqrt(jnp.mean(tok_rows * tok_rows, axis=-1, keepdims=True) + norm_eps)
    return tok_rows * inverse * gain_vec


def gelu_mix(gate_vals, up_vals):
    return jax.nn.gelu(gate_vals, approximate=True) * up_vals


def lookup(table, wanted):
    table_slots = jnp.arange(table.shape[0], dtype=jnp.int32)
    return jnp.sum(jnp.where(wanted[:, None] == table_slots[None, :], table[None, :], 0), axis=1)


def left_dot(lhs_mat, rhs_mat):
    return lax.dot_general(
        lhs_mat, rhs_mat, (((0,), (0,)), ((), ())), preferred_element_type=jnp.float32
    )


def right_dot(lhs_mat, rhs_mat):
    return lax.dot_general(
        lhs_mat, rhs_mat, (((1,), (1,)), ((), ())), preferred_element_type=jnp.float32
    )


def plain_dot(lhs_mat, rhs_mat):
    return jnp.dot(lhs_mat, rhs_mat, preferred_element_type=jnp.float32)


def attend_forward(queries, keys_all, values_all, live_keys):
    total_rows = queries.shape[0]
    row_block = min(512, total_rows)
    factor = HD ** (-0.5)
    key_heads = keys_all.reshape(total_rows, H, HD)
    value_heads = values_all.reshape(total_rows, H, HD)
    mixed_list = []
    stat_list = []
    for row_begin in range(0, total_rows, row_block):
        query_heads = queries[row_begin : row_begin + row_block].reshape(row_block, H, HD)
        scores = (
            jnp.einsum("qhd,khd->hqk", query_heads, key_heads, preferred_element_type=jnp.float32)
            * factor
        )
        scores = jnp.where(live_keys[None, None, :], scores, neg_big)
        row_max = jnp.max(scores, axis=-1, keepdims=True)
        exp_vals = jnp.exp(scores - row_max)
        row_total = jnp.sum(exp_vals, axis=-1, keepdims=True)
        prob_vals = (exp_vals / row_total).astype(jnp.bfloat16)
        mixed_rows = jnp.einsum(
            "hqk,khd->qhd", prob_vals, value_heads, preferred_element_type=jnp.float32
        )
        mixed_list.append(mixed_rows.reshape(row_block, H * HD))
        stat_list.append(row_max + jnp.log(row_total))
    return (jnp.concatenate(mixed_list, axis=0), jnp.concatenate(stat_list, axis=1))


def attend_backward(queries, keys_all, values_all, live_keys, log_totals, grad_mixed):
    total_rows = queries.shape[0]
    row_block = min(512, total_rows)
    factor = HD ** (-0.5)
    key_heads = keys_all.reshape(total_rows, H, HD)
    value_heads = values_all.reshape(total_rows, H, HD)
    grad_keys = jnp.zeros((total_rows, H, HD), jnp.float32)
    grad_values = jnp.zeros((total_rows, H, HD), jnp.float32)
    query_list = []
    for row_begin in range(0, total_rows, row_block):
        query_heads = queries[row_begin : row_begin + row_block].reshape(row_block, H, HD)
        grad_heads = grad_mixed[row_begin : row_begin + row_block].reshape(row_block, H, HD)
        scores = (
            jnp.einsum("qhd,khd->hqk", query_heads, key_heads, preferred_element_type=jnp.float32)
            * factor
        )
        scores = jnp.where(live_keys[None, None, :], scores, neg_big)
        prob_vals = jnp.exp(scores - log_totals[:, row_begin : row_begin + row_block])
        grad_probs = jnp.einsum(
            "qhd,khd->hqk", grad_heads, value_heads, preferred_element_type=jnp.float32
        )
        row_dot = jnp.sum(prob_vals * grad_probs, axis=-1, keepdims=True)
        grad_scores = (prob_vals * (grad_probs - row_dot)).astype(jnp.bfloat16)
        grad_query = (
            jnp.einsum("hqk,khd->qhd", grad_scores, key_heads, preferred_element_type=jnp.float32)
            * factor
        )
        query_list.append(grad_query.reshape(row_block, H * HD))
        grad_keys = (
            grad_keys
            + jnp.einsum(
                "hqk,qhd->khd", grad_scores, query_heads, preferred_element_type=jnp.float32
            )
            * factor
        )
        grad_values = grad_values + jnp.einsum(
            "hqk,qhd->khd",
            prob_vals.astype(jnp.bfloat16),
            grad_heads,
            preferred_element_type=jnp.float32,
        )
    return (
        jnp.concatenate(query_list, axis=0),
        grad_keys.reshape(total_rows, H * HD),
        grad_values.reshape(total_rows, H * HD),
    )


def shards(
    x_in,
    seq_units,
    deal,
    gain_attn,
    w_query,
    w_key,
    w_value,
    w_out,
    gain_ffn,
    w_gate,
    w_up,
    w_down,
    d_out,
):
    shard_count = lax.axis_size("shard")
    my_index = lax.axis_index("shard")
    width = x_in.shape[2]
    span = d_out.shape[2]
    unit_max = span // shard_count
    units_row = seq_units[0]
    order_row = deal[0]
    offsets = jnp.cumsum(units_row) - units_row
    inner_idx = jnp.arange(unit_max, dtype=jnp.int32)
    dest_idx = jnp.arange(shard_count, dtype=jnp.int32)
    counts = lookup(units_row, order_row)
    starts = lookup(offsets, order_row)
    row_index = starts[:, None] + jnp.minimum(inner_idx[None, :], counts[:, None] - 1)
    sent_live = inner_idx[None, :] < counts[:, None]
    local_rows = x_in[0]
    outgoing = jnp.where(
        sent_live[:, :, None], local_rows[row_index], jnp.zeros((), local_rows.dtype)
    )
    arrived = lax.all_to_all(outgoing, "shard", split_axis=0, concat_axis=0, tiled=True)
    own_count = jnp.sum(jnp.where(dest_idx == my_index, counts, 0))
    live_rows = jnp.broadcast_to(inner_idx[None, :] < own_count, (shard_count, unit_max)).reshape(
        span
    )
    wq_full, wk_full, wv_full, wo_full = (
        lax.all_gather(w_query, "shard", axis=0, tiled=True),
        lax.all_gather(w_key, "shard", axis=0, tiled=True),
        lax.all_gather(w_value, "shard", axis=0, tiled=True),
        lax.all_gather(w_out, "shard", axis=0, tiled=True),
    )
    tok_float = arrived.reshape(span, width).astype(jnp.float32)
    normed_one_f, norm_one_back = jax.vjp(rms_scale, tok_float, gain_attn)
    normed_one = normed_one_f.astype(jnp.bfloat16)
    queries = plain_dot(normed_one, wq_full).astype(jnp.bfloat16)
    keys_all = plain_dot(normed_one, wk_full).astype(jnp.bfloat16)
    values_all = plain_dot(normed_one, wv_full).astype(jnp.bfloat16)
    mixed_f, log_totals = attend_forward(queries, keys_all, values_all, live_rows)
    mixed_rows = mixed_f.astype(jnp.bfloat16)
    hidden_res = tok_float + plain_dot(mixed_rows, wo_full)
    wg_full, wu_full, wd_full = (
        lax.all_gather(w_gate, "shard", axis=0, tiled=True),
        lax.all_gather(w_up, "shard", axis=0, tiled=True),
        lax.all_gather(w_down, "shard", axis=0, tiled=True),
    )
    normed_two_f, norm_two_back = jax.vjp(rms_scale, hidden_res, gain_ffn)
    normed_two = normed_two_f.astype(jnp.bfloat16)
    gate_vals = plain_dot(normed_two, wg_full)
    up_vals = plain_dot(normed_two, wu_full)
    act_f, mix_back = jax.vjp(gelu_mix, gate_vals, up_vals)
    act_vals = act_f.astype(jnp.bfloat16)
    result = jnp.where(live_rows[:, None], hidden_res + plain_dot(act_vals, wd_full), 0.0)
    layer_out = result.astype(jnp.bfloat16).reshape(1, 1, span, width)
    wg_back, wu_back, wd_back = (
        lax.all_gather(w_gate, "shard", axis=0, tiled=True),
        lax.all_gather(w_up, "shard", axis=0, tiled=True),
        lax.all_gather(w_down, "shard", axis=0, tiled=True),
    )
    grad_y = jnp.where(live_rows[:, None], d_out[0, 0].astype(jnp.float32), 0.0)
    grad_ffn_b = grad_y.astype(jnp.bfloat16)
    grad_down = left_dot(act_vals, grad_ffn_b)
    grad_act = right_dot(grad_ffn_b, wd_back)
    grad_gate_f, grad_up_f = mix_back(grad_act)
    grad_gate_b = grad_gate_f.astype(jnp.bfloat16)
    grad_up_b = grad_up_f.astype(jnp.bfloat16)
    grad_wg = left_dot(normed_two, grad_gate_b)
    grad_wu = left_dot(normed_two, grad_up_b)
    grad_n2 = right_dot(grad_gate_b, wg_back) + right_dot(grad_up_b, wu_back)
    grad_h_norm, grad_gain_two = norm_two_back(grad_n2)
    ffn_share = (
        lax.psum_scatter(
            grad_wg.astype(jnp.bfloat16), "shard", scatter_dimension=0, tiled=True
        ).astype(jnp.float32),
        lax.psum_scatter(
            grad_wu.astype(jnp.bfloat16), "shard", scatter_dimension=0, tiled=True
        ).astype(jnp.float32),
        lax.psum_scatter(
            grad_down.astype(jnp.bfloat16), "shard", scatter_dimension=0, tiled=True
        ).astype(jnp.float32),
        lax.psum_scatter(
            grad_gain_two.astype(jnp.bfloat16), "shard", scatter_dimension=0, tiled=True
        ).astype(jnp.float32),
    )
    grad_hidden = grad_y + grad_h_norm
    wq_back, wk_back, wv_back, wo_back = (
        lax.all_gather(w_query, "shard", axis=0, tiled=True),
        lax.all_gather(w_key, "shard", axis=0, tiled=True),
        lax.all_gather(w_value, "shard", axis=0, tiled=True),
        lax.all_gather(w_out, "shard", axis=0, tiled=True),
    )
    grad_attn_b = grad_hidden.astype(jnp.bfloat16)
    grad_wo = left_dot(mixed_rows, grad_attn_b)
    grad_mixed = right_dot(grad_attn_b, wo_back).astype(jnp.bfloat16)
    grad_q_f, grad_k_f, grad_v_f = attend_backward(
        queries, keys_all, values_all, live_rows, log_totals, grad_mixed
    )
    grad_q_b = grad_q_f.astype(jnp.bfloat16)
    grad_k_b = grad_k_f.astype(jnp.bfloat16)
    grad_v_b = grad_v_f.astype(jnp.bfloat16)
    grad_wq = left_dot(normed_one, grad_q_b)
    grad_wk = left_dot(normed_one, grad_k_b)
    grad_wv = left_dot(normed_one, grad_v_b)
    grad_n1 = (
        right_dot(grad_q_b, wq_back) + right_dot(grad_k_b, wk_back) + right_dot(grad_v_b, wv_back)
    )
    grad_x_norm, grad_gain_one = norm_one_back(grad_n1)
    grad_tokens = (
        (grad_hidden + grad_x_norm).astype(jnp.bfloat16).reshape(shard_count, unit_max, width)
    )
    returned = lax.all_to_all(grad_tokens, "shard", split_axis=0, concat_axis=0, tiled=True)
    home_rows = (
        jnp.zeros(local_rows.shape, jnp.float32)
        .at[row_index]
        .add(jnp.where(sent_live[:, :, None], returned.astype(jnp.float32), 0.0))
    )
    grad_x = home_rows.astype(jnp.bfloat16)[None]
    attn_share = (
        lax.psum_scatter(
            grad_wq.astype(jnp.bfloat16), "shard", scatter_dimension=0, tiled=True
        ).astype(jnp.float32),
        lax.psum_scatter(
            grad_wk.astype(jnp.bfloat16), "shard", scatter_dimension=0, tiled=True
        ).astype(jnp.float32),
        lax.psum_scatter(
            grad_wv.astype(jnp.bfloat16), "shard", scatter_dimension=0, tiled=True
        ).astype(jnp.float32),
        lax.psum_scatter(
            grad_wo.astype(jnp.bfloat16), "shard", scatter_dimension=0, tiled=True
        ).astype(jnp.float32),
        lax.psum_scatter(
            grad_gain_one.astype(jnp.bfloat16), "shard", scatter_dimension=0, tiled=True
        ).astype(jnp.float32),
    )
    totals = (
        lax.psum(ffn_share[0].astype(jnp.bfloat16), "replica").astype(jnp.float32),
        lax.psum(ffn_share[1].astype(jnp.bfloat16), "replica").astype(jnp.float32),
        lax.psum(ffn_share[2].astype(jnp.bfloat16), "replica").astype(jnp.float32),
        lax.psum(ffn_share[3].astype(jnp.bfloat16), "replica").astype(jnp.float32),
        lax.psum(attn_share[0].astype(jnp.bfloat16), "replica").astype(jnp.float32),
        lax.psum(attn_share[1].astype(jnp.bfloat16), "replica").astype(jnp.float32),
        lax.psum(attn_share[2].astype(jnp.bfloat16), "replica").astype(jnp.float32),
        lax.psum(attn_share[3].astype(jnp.bfloat16), "replica").astype(jnp.float32),
        lax.psum(attn_share[4].astype(jnp.bfloat16), "replica").astype(jnp.float32),
    )
    return (
        layer_out,
        grad_x,
        totals[8],
        totals[3],
        totals[4],
        totals[5],
        totals[6],
        totals[7],
        totals[0],
        totals[1],
        totals[2],
    )


def solution(mesh):
    return jax.shard_map(
        shards,
        mesh=mesh,
        in_specs=(
            P("replica", "shard", None),
            P("replica", None),
            P("replica", None),
            P(),
            P("shard", None),
            P("shard", None),
            P("shard", None),
            P("shard", None),
            P(),
            P("shard", None),
            P("shard", None),
            P("shard", None),
            P("replica", "shard", None, None),
        ),
        out_specs=(
            P("replica", "shard", None, None),
            P("replica", "shard", None),
            P("shard"),
            P("shard"),
            P("shard", None),
            P("shard", None),
            P("shard", None),
            P("shard", None),
            P("shard", None),
            P("shard", None),
            P("shard", None),
        ),
        check_vma=False,
    )
```

profile of v0, /device:TPU:0, one launch (start us, length us, event | category | flops | bytes accessed | tf_op | source)
XLA Modules:
  0.0 894.3 jit_solution(441610172667195544)
XLA Ops:
  14.9 4.0 gather_fusion
  20.3 7.5 all-to-all-start
  29.4 35.4 %all-to-all-done = bf16[16,64,768]{2,1,0:T(8,128)(2,1)S(1)} async-done(((bf16[16,64,768]{2,1,0:T(8,128)(2,1)}), bf16[16,64,768]{2,1,0:T(8,128)(2,1)S(1)}, u32[]{:S(2)}, u32[]{:S(2)}) %all-to-all-start) | async-done | bytes 1572896 | tf_op jit(solution)/shard_map/all_to_all | solution.py:150
  66.8 3.2 convolution_convert_fusion.5
  70.1 33.1 %all-gather.12.cloned.1.call-done = bf16[768,768]{1,0:T(8,128)(2,1)} async-done(((bf16[48,768]{1,0:T(8,128)(2,1)}), bf16[768,768]{1,0:T(8,128)(2,1)}) %all-gather.12.cloned.1.call-update) | async-done | bytes 1179664 | tf_op jit(solution)/shard_map/all_gather | solution.py:157
  103.3 3.2 convolution_convert_fusion.4
  106.5 10.7 %fusion.65 = f32[12,512,1024]{2,1,0:T(8,128)} fusion(bf16[512,12,64]{0,2,1:T(8,128)(2,1)S(1)} %bitcast.124, bf16[1024,12,64]{0,2,1:T(8,128)(2,1)S(1)} %bitcast.120), kind=kOutput, calls=%fused_computation.130 | convolution fusion | flops 805306368 | bytes 27525120 | tf_op jit(solution)/shard_map/qhd,khd->hqk/dot_general | solution.py:53
  117.2 16.7 %fusion.12 = (f32[12,512]{1,0:T(8,128)S(1)}, f32[12,512]{1,0:T(8,128)S(1)}, f32[12,512,1024]{2,1,0:T(8,128)}) fusion(pred[1024]{0:T(1024)(128)(4,1)S(1)} %broadcast_in_dim.135, f32[12,512,1024]{2,1,0:T(8,128)} %fusion.65, bf16[512,12,64]{0,2,1:T(8,128)(2,1)S(1)} %bitcast.130, bf16[1024,12,64]{0,2,1:T(8,128)(2,1)} %bitcast.121), kind=kOutput, calls=%fused_computation.26 | convolution fusion | flops 843042816 | bytes 52741120 | tf_op jit(solution)/shard_map/qhd,khd->hqk/dot_general | solution.py:53
  133.9 18.7 %fusion = (f32[12,512]{1,0:T(8,128)S(1)}, f32[12,512]{1,0:T(8,128)S(1)}) fusion(f32[12,512]{1,0:T(8,128)S(1)} %get-tuple-element.19, f32[12,512,1024]{2,1,0:T(8,128)} %get-tuple-element.47, pred[1024]{0:T(1024)(128)(4,1)S(1)} %broadcast_in_dim.135, f32[12,512]{1,0:T(8,128)S(1)} %get-tuple-element.20, f32[12,512,1024]{2,1,0:T(8,128)} %fusion.65), kind=kLoop, calls=%fused_computation.14 | loop fusion | flops 50319360 | bytes 50430976 | tf_op jit(solution)/shard_map/reduce_sum | solution.py:59
  152.6 3.2 convolution_convert_fusion.6
  155.8 11.7 %fusion.37 = bf16[12,64,512]{2,1,0:T(8,128)(2,1)S(1)} fusion(bf16[1024,12,64]{0,2,1:T(8,128)(2,1)S(1)} %bitcast.126, f32[12,512]{1,0:T(8,128)S(1)} %get-tuple-element.17, f32[12,512]{1,0:T(8,128)S(1)} %get-tuple-element.19, f32[12,512,1024]{2,1,0:T(8,128)} %get-tuple-element.47, pred[1024]{0:T(1024)(128)(4,1)S(1)} %broadcast_in_dim.135), kind=kOutput, calls=%fused_computation.87 | convolution fusion | flops 837156864 | bytes 27575296 | tf_op jit(solution)/shard_map/hqk,khd->qhd/dot_general | solution.py:61
  167.6 12.2 %fusion.36 = bf16[12,64,512]{2,1,0:T(8,128)(2,1)} fusion(bf16[1024,12,64]{0,2,1:T(8,128)(2,1)S(1)} %bitcast.127, f32[12,512]{1,0:T(8,128)S(1)} %get-tuple-element.18, f32[12,512]{1,0:T(8,128)S(1)} %get-tuple-element.20, f32[12,512,1024]{2,1,0:T(8,128)} %fusion.65, pred[1024]{0:T(1024)(128)(4,1)S(1)} %broadcast_in_dim.135), kind=kOutput, calls=%fused_computation.86 | convolution fusion | flops 837156864 | bytes 27575296 | tf_op jit(solution)/shard_map/hqk,khd->qhd/dot_general | solution.py:61
  182.1 3.2 multiply_reduce_fusion.4
  187.8 40.9 %all-gather.18.cloned.1.call-done = bf16[768,2048]{1,0:T(8,128)(2,1)} async-done(((bf16[48,2048]{1,0:T(8,128)(2,1)}), bf16[768,2048]{1,0:T(8,128)(2,1)}) %all-gather.18.cloned.1.call-update) | async-done | bytes 3145744 | tf_op jit(solution)/shard_map/all_gather | solution.py:172
  228.7 7.5 fusion.67
  236.1 38.5 %all-gather.16.cloned.1.call-done = bf16[768,2048]{1,0:T(8,128)(2,1)} async-done(((bf16[48,2048]{1,0:T(8,128)(2,1)}), bf16[768,2048]{1,0:T(8,128)(2,1)}) %all-gather.16.cloned.1.call-update) | async-done | bytes 3145744 | tf_op jit(solution)/shard_map/all_gather | solution.py:171
  274.7 9.0 %fusion.66 = f32[1024,2048]{1,0:T(8,128)} fusion(bf16[1024,768]{1,0:T(8,128)(2,1)} %copy-done.22, bf16[768,2048]{1,0:T(8,128)(2,1)} %all-gather.16.cloned.1.call-done), kind=kOutput, calls=%fused_computation.131 | convolution fusion | flops 3221225472 | bytes 13107200 | tf_op jit(solution)/shard_map/dot_general | solution.py:39
  283.7 37.1 %all-gather.20.cloned.1.call-done = bf16[2048,768]{1,0:T(8,128)(2,1)} async-done(((bf16[128,768]{1,0:T(8,128)(2,1)}), bf16[2048,768]{1,0:T(8,128)(2,1)}) %all-gather.20.cloned.1.call-update) | async-done | bytes 3145744 | tf_op jit(solution)/shard_map/all_gather | solution.py:173
  320.8 15.1 %multiply_convert_fusion.2 = (bf16[1024,2048]{1,0:T(8,128)(2,1)S(1)}, bf16[1024,2048]{1,0:T(8,128)(2,1)}, bf16[1024,2048]{1,0:T(8,128)(2,1)}) fusion(f32[1024,2048]{1,0:T(8,128)} %fusion.66, f32[1024,2048]{1,0:T(8,128)} %fusion.67, bf16[2048,768]{1,0:T(8,128)(2,1)} %all-gather.20.cloned.1.call-done, bf16[1,1,1024,768]{3,2,1,0:T(8,128)(2,1)S(1)} %copy-done.16, ...), kind=kOutput, calls=%fused_computation.35 | convolution fusion | flops 3278110720 | bytes 34079744 | tf_op jit(solution)/shard_map/dot_general | solution.py:33
  335.9 7.3 fusion.68
  343.2 4.6 multiply_reduce_fusion.2
  350.8 2.5 convolution_convert_fusion.7
  353.4 3.3 convolution_convert_fusion.3
  358.1 10.8 %fusion.69 = f32[12,512,1024]{2,1,0:T(8,128)} fusion(bf16[512,12,64]{0,2,1:T(8,128)(2,1)S(1)} %bitcast.132, bf16[1024,12,64]{0,2,1:T(8,128)(2,1)S(1)} %bitcast.128), kind=kOutput, calls=%fused_computation.134 | convolution fusion | flops 805306368 | bytes 27525120 | tf_op jit(solution)/shard_map/qhd,khd->hqk/dot_general | solution.py:87
  368.9 12.6 %fusion.4 = f32[12,64,1024]{2,1,0:T(8,128)} fusion(bf16[512,12,64]{0,2,1:T(8,128)(2,1)S(1)} %bitcast.133, f32[12,512]{1,0:T(8,128)S(1)} %get-tuple-element.53, f32[12,512,1024]{2,1,0:T(8,128)} %fusion.65, pred[1024]{0:T(1024)(128)(4,1)S(1)} %broadcast_in_dim.135), kind=kOutput, calls=%fused_computation.18 | convolution fusion | flops 830472192 | bytes 29123584 | tf_op jit(solution)/shard_map/hqk,qhd->khd/dot_general | solution.py:104
  381.5 35.6 %multiply_reduce_fusion.1 = (f32[12,512]{1,0:T(8,128)S(1)}, f32[12,512]{1,0:T(8,128)S(1)}, f32[12,512,1024]{2,1,0:T(8,128)}) fusion(f32[12,512]{1,0:T(8,128)S(1)} %get-tuple-element.54, f32[12,512,1024]{2,1,0:T(8,128)} %get-tuple-element.47, pred[1024]{0:T(1024)(128)(4,1)S(1)} %broadcast_in_dim.135, f32[12,512,1024]{2,1,0:T(8,128)} %fusion.69, ...), kind=kOutput, calls=%fused_computation.6 | convolution fusion | flops 868208640 | bytes 103121920 | tf_op jit(solution)/shard_map/qhd,khd->hqk/dot_general | solution.py:87
  417.1 12.3 %add_convert_fusion = bf16[12,64,1024]{2,1,0:T(8,128)(2,1)S(1)} fusion(f32[12,64,1024]{2,1,0:T(8,128)} %fusion.4, bf16[512,12,64]{0,2,1:T(8,128)(2,1)S(1)} %bitcast.138, f32[12,512]{1,0:T(8,128)S(1)} %get-tuple-element.54, f32[12,512,1024]{2,1,0:T(8,128)} %get-tuple-element.47, pred[1024]{0:T(1024)(128)(4,1)S(1)} %broadcast_in_dim.135), kind=kOutput, calls=%fused_computation.64 | convolution fusion | flops 832045056 | bytes 30696448 | tf_op jit(solution)/shard_map/hqk,qhd->khd/dot_general | solution.py:104
  430.6 2.5 convolution_convert_fusion.8
  433.1 42.5 %multiply_convert_fusion.1 = (bf16[12,512,1024]{2,1,0:T(8,128)(2,1)}, bf16[12,512,1024]{2,1,0:T(8,128)(2,1)}) fusion(f32[12,512,1024]{2,1,0:T(8,128)} %get-tuple-element.51, f32[12,512]{1,0:T(8,128)S(1)} %get-tuple-element.15, f32[12,512]{1,0:T(8,128)S(1)} %get-tuple-element.54, f32[12,512,1024]{2,1,0:T(8,128)} %get-tuple-element.47, ...), kind=kLoop, calls=%fused_computation.5 | loop fusion | flops 75497472 | bytes 125928448 | tf_op jit(solution)/shard_map/convert_element_type | solution.py:91
  475.7 8.6 multiply_convert_fusion.7
  484.3 8.7 multiply_convert_fusion.6
  495.7 6.9 fusion.70
  502.7 7.2 multiply_convert_fusion.4
  509.9 2.5 convolution_convert_fusion.9
  512.5 7.9 convolution_convert_fusion
  520.5 7.9 convolution_convert_fusion.2
  528.8 7.8 convolution_convert_fusion.1
  537.8 2.8 fusion.38
  542.8 2.5 fusion.28
  547.3 3.8 all-to-all-start.1
  552.7 60.4 %reduce-scatter.10.cloned.1.call-done = bf16[48,768]{1,0:T(8,128)(2,1)} async-done(((bf16[768,768]{1,0:T(8,128)(2,1)}), bf16[48,768]{1,0:T(8,128)(2,1)}) %reduce-scatter.10.cloned.1.call-update) | async-done | bytes 73744 | tf_op jit(solution)/shard_map/reduce_scatter | solution.py:250
  613.1 69.0 %reduce-scatter.20.cloned.1.call-done = bf16[128,768]{1,0:T(8,128)(2,1)} async-done(((bf16[2048,768]{1,0:T(8,128)(2,1)}), bf16[128,768]{1,0:T(8,128)(2,1)}) %reduce-scatter.20.cloned.1.call-update) | async-done | bytes 196624 | tf_op jit(solution)/shard_map/reduce_scatter | solution.py:206
  682.2 69.1 %reduce-scatter.16.cloned.1.call-done = bf16[48,2048]{1,0:T(8,128)(2,1)} async-done(((bf16[768,2048]{1,0:T(8,128)(2,1)}), bf16[48,2048]{1,0:T(8,128)(2,1)}) %reduce-scatter.16.cloned.1.call-update) | async-done | bytes 196624 | tf_op jit(solution)/shard_map/reduce_scatter | solution.py:200
  751.3 69.1 %reduce-scatter.18.cloned.1.call-done = bf16[48,2048]{1,0:T(8,128)(2,1)} async-done(((bf16[768,2048]{1,0:T(8,128)(2,1)}), bf16[48,2048]{1,0:T(8,128)(2,1)}) %reduce-scatter.18.cloned.1.call-update) | async-done | bytes 196624 | tf_op jit(solution)/shard_map/reduce_scatter | solution.py:203
  820.5 8.6 fusion.35
  829.1 29.5 %all-reduce.2 = (bf16[768]{0:T(1024)(128)(2,1)S(1)}, bf16[768]{0:T(1024)(128)(2,1)S(1)}) all-reduce(bf16[768]{0:T(1024)(128)(2,1)S(1)} %get-tuple-element.13, bf16[768]{0:T(1024)(128)(2,1)S(1)} %copy-done.36), channel_id=2, replica_groups=mesh['shard'=16,'replica'=2] {'shard'}, use_global_device_ids=true, to_apply=%region_16.17.clone | all-reduce | flops 1536 | bytes 6144
  858.8 4.9 all-reduce.3
  866.7 8.6 scatter_custom_fusion
  (169 shorter events, 48.2 us)
Async XLA Ops:
  7.2 7.7 copy-start
  7.2 59.6 %all-gather.10.cloned.1.call-start = ((), (), s32[]{:S(2)}) async-start(), calls=%async_computation.10 | async-start | bytes 1253376 | tf_op jit(solution)/shard_map/all_gather | solution.py:156
  7.9 95.3 %all-gather.12.cloned.1.call-start = ((), (), s32[]{:S(2)}) async-start(), calls=%async_computation.11 | async-start | bytes 1253376 | tf_op jit(solution)/shard_map/all_gather | solution.py:157
  8.7 143.9 %all-gather.8.cloned.1.call-start = ((), (), s32[]{:S(2)}) async-start(), calls=%async_computation.9 | async-start | bytes 1253376 | tf_op jit(solution)/shard_map/all_gather | solution.py:158
  9.4 172.7 %all-gather.14.cloned.1.call-start = ((), (), s32[]{:S(2)}) async-start(), calls=%async_computation.12 | async-start | bytes 1253376 | tf_op jit(solution)/shard_map/all_gather | solution.py:159
  10.0 218.7 %all-gather.18.cloned.1.call-start = ((), (), s32[]{:S(2)}) async-start(), calls=%async_computation.14 | async-start | bytes 3342336 | tf_op jit(solution)/shard_map/all_gather | solution.py:172
  10.6 264.1 %all-gather.16.cloned.1.call-start = ((), (), s32[]{:S(2)}) async-start(), calls=%async_computation.13 | async-start | bytes 3342336 | tf_op jit(solution)/shard_map/all_gather | solution.py:171
  20.3 44.9 %copy-start.26 = (f32[768]{0:T(1024)S(1)}, f32[768]{0:T(1024)}, u32[]{:S(2)}) copy-start(f32[768]{0:T(1024)} %param.16) | copy-start | bytes 9220
  20.3 44.4 %all-to-all-start = ((bf16[16,64,768]{2,1,0:T(8,128)(2,1)}), bf16[16,64,768]{2,1,0:T(8,128)(2,1)S(1)}, u32[]{:S(2)}, u32[]{:S(2)}) async-start(bf16[16,64,768]{2,1,0:T(8,128)(2,1)} %broadcast_select_fusion), calls=%async_computation | async-start | bytes 3145728 | tf_op jit(solution)/shard_map/all_to_all | solution.py:150
  27.9 292.9 %all-gather.20.cloned.1.call-start = ((), (), s32[]{:S(2)}) async-start(), calls=%async_computation.15 | async-start | bytes 3342336 | tf_op jit(solution)/shard_map/all_gather | solution.py:173
  28.6 524.1 %reduce-scatter.14.cloned.1.call-start = ((), (), s32[]{:S(2)}) async-start(), calls=%async_computation.19 | async-start | bytes 1253376 | tf_op jit(solution)/shard_map/reduce_scatter | solution.py:256
  64.8 120.6 %copy-start.2 = (bf16[16,64,768]{2,1,0:T(8,128)(2,1)}, bf16[16,64,768]{2,1,0:T(8,128)(2,1)S(1)}, u32[]{:S(2)}) copy-start(bf16[16,64,768]{2,1,0:T(8,128)(2,1)S(1)} %all-to-all-done) | copy-start | bytes 4718596
  70.1 36.3 %copy-start.6 = (bf16[512,768]{0,1:T(8,128)(2,1)}, bf16[512,768]{0,1:T(8,128)(2,1)S(1)}, u32[]{:S(2)}) copy-start(bf16[512,768]{0,1:T(8,128)(2,1)S(1)} %get-tuple-element.39) | copy-start | bytes 2359300
  70.1 47.1 %copy-start.14 = (bf16[512,768]{0,1:T(8,128)(2,1)}, bf16[512,768]{0,1:T(8,128)(2,1)S(1)}, u32[]{:S(2)}) copy-start(bf16[512,768]{0,1:T(8,128)(2,1)S(1)} %get-tuple-element.40) | copy-start | bytes 2359300
  106.5 10.8 %copy-start.4 = (bf16[1024,768]{0,1:T(8,128)(2,1)}, bf16[1024,768]{0,1:T(8,128)(2,1)S(1)}, u32[]{:S(2)}) copy-start(bf16[1024,768]{0,1:T(8,128)(2,1)S(1)} %convolution_convert_fusion.4) | copy-start | bytes 4718596
  155.8 11.7 %copy-start.8 = (bf16[1024,768]{0,1:T(8,128)(2,1)}, bf16[1024,768]{0,1:T(8,128)(2,1)S(1)}, u32[]{:S(2)}) copy-start(bf16[1024,768]{0,1:T(8,128)(2,1)S(1)} %convolution_convert_fusion.6) | copy-start | bytes 4718596
  187.8 40.9 %copy-start.22 = (bf16[1024,768]{1,0:T(8,128)(2,1)}, bf16[1024,768]{1,0:T(8,128)(2,1)S(1)}, u32[]{:S(2)}) copy-start(bf16[1024,768]{1,0:T(8,128)(2,1)S(1)} %multiply_convert_fusion.5) | copy-start | bytes 4718596
  236.1 84.7 %copy-start.16 = (bf16[1,1,1024,768]{3,2,1,0:T(8,128)(2,1)S(1)}, bf16[1,1,1024,768]{3,2,1,0:T(8,128)(2,1)}, u32[]{:S(2)}) copy-start(bf16[1,1,1024,768]{3,2,1,0:T(8,128)(2,1)} %param.25) | copy-start | bytes 4718596
  320.8 15.1 %copy-start.38 = (bf16[768,2048]{1,0:T(8,128)(2,1)S(1)}, bf16[768,2048]{1,0:T(8,128)(2,1)}, u32[]{:S(2)}) copy-start(bf16[768,2048]{1,0:T(8,128)(2,1)} %all-gather.16.cloned.1.call-done) | copy-start | bytes 9437188
  335.9 7.3 copy-start.43
  335.9 7.3 copy-start.13
  335.9 7.3 copy-start.37
  347.8 3.0 copy-start.41
  350.8 2.6 copy-start.40
  353.3 199.4 %reduce-scatter.12.cloned.1.call-start = ((), (), s32[]{:S(2)}) async-start(), calls=%async_computation.18 | async-start | bytes 1253376 | tf_op jit(solution)/shard_map/reduce_scatter | solution.py:253
  417.1 13.5 %copy-start.20 = (bf16[16,64,768]{2,1,0:T(8,128)(2,1)S(1)}, bf16[16,64,768]{2,1,0:T(8,128)(2,1)}, u32[]{:S(2)}) copy-start(bf16[16,64,768]{2,1,0:T(8,128)(2,1)} %fusion.31) | copy-start | bytes 4718596
  433.1 119.6 %reduce-scatter.8.cloned.1.call-start = ((), (), s32[]{:S(2)}) async-start(), calls=%async_computation.16 | async-start | bytes 1253376 | tf_op jit(solution)/shard_map/reduce_scatter | solution.py:247
  433.1 42.6 %copy-start.5 = (bf16[1024,768]{0,1:T(8,128)(2,1)S(1)}, bf16[1024,768]{0,1:T(8,128)(2,1)}, u32[]{:S(2)}) copy-start(bf16[1024,768]{0,1:T(8,128)(2,1)} %copy-done.4) | copy-start | bytes 4718596
  484.3 8.7 copy-start.19
  492.9 2.5 copy-start.24
  492.9 2.8 copy-start.15
  495.4 7.2 copy-start.7
  495.4 117.7 %reduce-scatter.10.cloned.1.call-start = ((), (), s32[]{:S(2)}) async-start(), calls=%async_computation.17 | async-start | bytes 1253376 | tf_op jit(solution)/shard_map/reduce_scatter | solution.py:250
  502.6 7.3 copy-start.21
  512.4 169.8 %reduce-scatter.20.cloned.1.call-start = ((), (), s32[]{:S(2)}) async-start(), calls=%async_computation.22 | async-start | bytes 3342336 | tf_op jit(solution)/shard_map/reduce_scatter | solution.py:206
  520.4 230.9 %reduce-scatter.16.cloned.1.call-start = ((), (), s32[]{:S(2)}) async-start(), calls=%async_computation.20 | async-start | bytes 3342336 | tf_op jit(solution)/shard_map/reduce_scatter | solution.py:200
  528.4 292.1 %reduce-scatter.18.cloned.1.call-start = ((), (), s32[]{:S(2)}) async-start(), calls=%async_computation.21 | async-start | bytes 3342336 | tf_op jit(solution)/shard_map/reduce_scatter | solution.py:203
  537.8 2.8 copy-start.39
  540.6 2.2 copy-start.23
  540.6 2.2 copy-start.27
  542.8 2.5 copy-start.31
  542.8 2.5 copy-start.11
  547.3 4.1 copy-start.42
  547.3 317.4 %all-to-all-start.1 = ((bf16[16,64,768]{2,1,0:T(8,128)(2,1)}), bf16[16,64,768]{2,1,0:T(8,128)(2,1)S(1)}, u32[]{:S(2)}, u32[]{:S(2)}) async-start(bf16[16,64,768]{2,1,0:T(8,128)(2,1)} %bitcast.26), calls=%async_computation.1 | async-start | bytes 3145728 | tf_op jit(solution)/shard_map/all_to_all | solution.py:239
  551.2 325.1 %all-reduce.7.cloned.1.call-start = ((), (), s32[]{:S(2)}) async-start(), calls=%async_computation.23 | async-start | bytes 1769472 | tf_op jit(solution)/shard_map/psum | solution.py:268
  820.5 8.6 copy-start.36
  820.5 44.2 %copy-start.33 = (pred[16,64]{1,0:T(8,128)(4,1)S(1)}, pred[16,64]{1,0:T(8,128)(4,1)}, u32[]{:S(2)}) copy-start(pred[16,64]{1,0:T(8,128)(4,1)} %copy-done.32) | copy-start | bytes 3076
  866.7 20.9 %copy-start.1 = (bf16[1,512,768]{2,1,0:T(8,128)(2,1)S(1)}, bf16[1,512,768]{2,1,0:T(8,128)(2,1)}, u32[]{:S(2)}) copy-start(bf16[1,512,768]{2,1,0:T(8,128)(2,1)} %param.13) | copy-start | bytes 2359300
  (13 other events, 20.5 us)
Sparse Core Ops, SparseCore 0:
  10.3 51.5 all-gather.9
  64.1 39.0 all-gather.11
  105.6 37.1 all-gather.7
  144.9 37.1 all-gather.13
  184.2 44.3 all-gather.17
  230.8 43.8 all-gather.15
  276.9 43.8 all-gather.19
  353.5 56.5 reduce-scatter.13
  433.2 56.6 reduce-scatter.11
  495.5 56.5 reduce-scatter.7
  555.8 57.3 reduce-scatter.9
  616.8 65.3 reduce-scatter.19
  686.0 65.2 reduce-scatter.15
  755.0 65.4 reduce-scatter.17
  823.0 35.4 all-reduce.6
where the time goes:
time: 900 us; the launch traced here: 894 us
  waiting for transfers between devices  460 us (51%)
  matrix products  262 us (29%)
  other arithmetic  97.7 us (11%)
  blocking collectives  34.4 us (4%)
  between operations  15.4 us (2%)
  starting transfers between devices  12.7 us (1%)
  local copies, waits for them, and re-layouts  12.1 us (1%)
    reduce_scatter x1, waiting for transfers between devices, shards(): lax.psum_scatter(grad_wg.astype(jnp.bfloat16), 'shard', scatter_dimension...  69.1 us
    reduce_scatter x1, waiting for transfers between devices, shards(): lax.psum_scatter(grad_wu.astype(jnp.bfloat16), 'shard', scatter_dimension...  69.1 us
    reduce_scatter x1, waiting for transfers between devices, shards(): lax.psum_scatter(grad_down.astype(jnp.bfloat16), 'shard', scatter_dimensi...  69 us
    reduce_scatter x1, waiting for transfers between devices, shards(): lax.psum_scatter(grad_wk.astype(jnp.bfloat16), 'shard', scatter_dimension...  60.4 us
    dot_general x2, matrix products, attend_backward(): jnp.einsum('qhd,khd->hqk', grad_heads, value_heads, preferred_element_typ...  46.4 us
    convert_element_type x1, other arithmetic, attend_backward(): grad_scores = (prob_vals * (grad_probs - row_dot)).astype(jnp.bfloat16)  42.5 us
    all_gather x1, waiting for transfers between devices, shards(): lax.all_gather(w_up, 'shard', axis=0, tiled=True)  40.9 us
    all_gather x1, waiting for transfers between devices, shards(): lax.all_gather(w_gate, 'shard', axis=0, tiled=True)  38.5 us
  transfers between devices with their start and end apart: 17, of which 10 were waited for; matrix products, arithmetic and copies ran while one was open for 36% of the time, Pallas kernels for 0%

commit v1 on v0

--- a/solution.py
+++ b/solution.py
@@ -7,6 +7,18 @@
 HD = 64
 norm_eps = 1e-06
 neg_big = -1e30
+
+
+def split_up(x, dim, size):
+    shape = x.shape
+    pieces = x.reshape(*shape[:dim], size, shape[dim] // size, *shape[dim + 1 :])
+    return jnp.moveaxis(pieces, dim, 0)
+
+
+def laid_out(blocks, dim):
+    blocks = jnp.moveaxis(blocks, 0, dim)
+    shape = blocks.shape
+    return blocks.reshape(*shape[:dim], shape[dim] * shape[dim + 1], *shape[dim + 2 :])
 
 
 def rms_scale(tok_rows, gain_vec):
@@ -147,7 +159,14 @@
     outgoing = jnp.where(
         sent_live[:, :, None], local_rows[row_index], jnp.zeros((), local_rows.dtype)
     )
-    arrived = lax.all_to_all(outgoing, "shard", split_axis=0, concat_axis=0, tiled=True)
+    peers, index = (lax.axis_size("shard"), lax.axis_index("shard"))
+    tiles = split_up(outgoing, 0, peers)
+    outs = [tiles[index]]
+    for turn in range(1, peers):
+        sent = tiles[index ^ turn]
+        outs.append(lax.ppermute(sent, "shard", [(i, i ^ turn) for i in range(peers)]))
+    tiles = jnp.stack(outs)[index ^ jnp.arange(peers)]
+    arrived = laid_out(tiles, 0)
     own_count = jnp.sum(jnp.where(dest_idx == my_index, counts, 0))
     live_rows = jnp.broadcast_to(inner_idx[None, :] < own_count, (shard_count, unit_max)).reshape(
         span

time: 900 us -> 901 us (level)
  waiting for transfers between devices: 460 us -> 443 us
  starting transfers between devices: 12.7 us -> 23.2 us
    ppermute x0 -> x15, waiting for transfers between devices: none -> 58.2 us  [shards(): lax.ppermute(sent, 'shard', [(i, i ^ turn) for i in range(peers)])]
    all_to_all x1 -> x0, waiting for transfers between devices: 35.4 us -> none  [shards(): lax.all_to_all(outgoing, 'shard', split_axis=0, concat_axis=0, tiled=True)]
    all_gather x1, waiting for transfers between devices: 33.1 us -> 0.02 us  [shards(): lax.all_gather(w_key, 'shard', axis=0, tiled=True)]
    ppermute x0 -> x15, starting transfers between devices: none -> 18 us  [shards(): lax.ppermute(sent, 'shard', [(i, i ^ turn) for i in range(peers)])]
  transfers between devices with their start and end apart: 17 -> 31, of which waited for: 10 -> 17; matrix products, arithmetic and copies ran while one was open for 36% -> 36% of each run, Pallas kernels for 0% -> 0%
where the time goes in v1:
time: 901 us; the launch traced here: 895 us
  waiting for transfers between devices  443 us (49%)
  matrix products  263 us (29%)
  other arithmetic  96.5 us (11%)
  blocking collectives  34.4 us (4%)
  starting transfers between devices  23.2 us (3%)
  local copies, waits for them, and re-layouts  19.1 us (2%)
  between operations  15.6 us (2%)
    reduce_scatter x1, waiting for transfers between devices, shards(): lax.psum_scatter(grad_wg.astype(jnp.bfloat16), 'shard', scatter_dimension...  69.1 us
    reduce_scatter x1, waiting for transfers between devices, shards(): lax.psum_scatter(grad_down.astype(jnp.bfloat16), 'shard', scatter_dimensi...  69 us
    reduce_scatter x1, waiting for transfers between devices, shards(): lax.psum_scatter(grad_wu.astype(jnp.bfloat16), 'shard', scatter_dimension...  69 us
    reduce_scatter x1, waiting for transfers between devices, shards(): lax.psum_scatter(grad_wk.astype(jnp.bfloat16), 'shard', scatter_dimension...  60.5 us
    ppermute x15, waiting for transfers between devices, shards(): lax.ppermute(sent, 'shard', [(i, i ^ turn) for i in range(peers)])  58.2 us
    dot_general x2, matrix products, attend_backward(): jnp.einsum('qhd,khd->hqk', grad_heads, value_heads, preferred_element_typ...  46.4 us
    convert_element_type x1, other arithmetic, attend_backward(): grad_scores = (prob_vals * (grad_probs - row_dot)).astype(jnp.bfloat16)  42.7 us
    all_gather x1, waiting for transfers between devices, shards(): lax.all_gather(w_gate, 'shard', axis=0, tiled=True)  38.5 us
  transfers between devices with their start and end apart: 31, of which 17 were waited for; matrix products, arithmetic and copies ran while one was open for 36% of the time, Pallas kernels for 0%

profile of v1, /device:TPU:0, one launch (start us, length us, event | category | flops | bytes accessed | tf_op | source)
XLA Modules:
  0.0 894.9 jit_solution(13076250737856059809)
XLA Ops:
  15.0 4.0 gather_fusion
  20.6 5.5 collective-permute-start.14
  33.5 3.8 collective-permute-done.1
  38.0 4.3 collective-permute-done.2
  42.7 4.3 collective-permute-done.3
  47.1 5.2 collective-permute-done.4
  54.2 4.5 collective-permute-done.5
  58.8 5.2 collective-permute-done.6
  64.0 3.8 collective-permute-start.7
  67.8 4.8 collective-permute-done.7
  72.6 9.1 %collective-permute-done.8 = bf16[1,64,768]{2,1,0:T(8,128)(2,1)S(1)} collective-permute-done((bf16[1,64,768]{2,1,0:T(8,128)(2,1)S(1)}, bf16[1,64,768]{2,1,0:T(8,128)(2,1)S(1)}, u32[]{:S(2)}, u32[]{:S(2)}) %collective-permute-start.8) | collective-permute-done | bytes 98336 | tf_op jit(solution)/shard_map/ppermute | solution.py:167
  81.8 6.7 collective-permute-done.9
  88.5 10.2 %collective-permute-done.10 = bf16[1,64,768]{2,1,0:T(8,128)(2,1)S(1)} collective-permute-done((bf16[1,64,768]{2,1,0:T(8,128)(2,1)S(1)}, bf16[1,64,768]{2,1,0:T(8,128)(2,1)S(1)}, u32[]{:S(2)}, u32[]{:S(2)}) %collective-permute-start.10) | collective-permute-done | bytes 98336 | tf_op jit(solution)/shard_map/ppermute | solution.py:167
  109.0 3.7 convolution_convert_fusion.4
  112.7 10.7 %fusion.66 = f32[12,512,1024]{2,1,0:T(8,128)} fusion(bf16[512,12,64]{0,2,1:T(8,128)(2,1)S(1)} %bitcast.168, bf16[1024,12,64]{0,2,1:T(8,128)(2,1)S(1)} %bitcast.164), kind=kOutput, calls=%fused_computation.165 | convolution fusion | flops 805306368 | bytes 27525120 | tf_op jit(solution)/shard_map/qhd,khd->hqk/dot_general | solution.py:65
  123.4 16.7 %fusion.12 = (f32[12,512]{1,0:T(8,128)S(1)}, f32[12,512]{1,0:T(8,128)S(1)}, f32[12,512,1024]{2,1,0:T(8,128)}) fusion(pred[1024]{0:T(1024)(128)(4,1)S(1)} %broadcast_in_dim.138, f32[12,512,1024]{2,1,0:T(8,128)} %fusion.66, bf16[512,12,64]{0,2,1:T(8,128)(2,1)S(1)} %bitcast.174, bf16[1024,12,64]{0,2,1:T(8,128)(2,1)} %bitcast.165), kind=kOutput, calls=%fused_computation.27 | convolution fusion | flops 843042816 | bytes 52741120 | tf_op jit(solution)/shard_map/qhd,khd->hqk/dot_general | solution.py:65
  140.1 18.7 %fusion = (f32[12,512]{1,0:T(8,128)S(1)}, f32[12,512]{1,0:T(8,128)S(1)}) fusion(f32[12,512]{1,0:T(8,128)S(1)} %get-tuple-element.19, f32[12,512,1024]{2,1,0:T(8,128)} %get-tuple-element.62, pred[1024]{0:T(1024)(128)(4,1)S(1)} %broadcast_in_dim.138, f32[12,512]{1,0:T(8,128)S(1)} %get-tuple-element.20, f32[12,512,1024]{2,1,0:T(8,128)} %fusion.66), kind=kLoop, calls=%fused_computation.15 | loop fusion | flops 50319360 | bytes 50430976 | tf_op jit(solution)/shard_map/reduce_sum | solution.py:71
  162.0 11.7 %fusion.37 = bf16[12,64,512]{2,1,0:T(8,128)(2,1)S(1)} fusion(bf16[1024,12,64]{0,2,1:T(8,128)(2,1)S(1)} %bitcast.170, f32[12,512]{1,0:T(8,128)S(1)} %get-tuple-element.17, f32[12,512]{1,0:T(8,128)S(1)} %get-tuple-element.19, f32[12,512,1024]{2,1,0:T(8,128)} %get-tuple-element.62, pred[1024]{0:T(1024)(128)(4,1)S(1)} %broadcast_in_dim.138), kind=kOutput, calls=%fused_computation.88 | convolution fusion | flops 837156864 | bytes 27575296 | tf_op jit(solution)/shard_map/hqk,khd->qhd/dot_general | solution.py:73
  173.7 12.3 %fusion.36 = bf16[12,64,512]{2,1,0:T(8,128)(2,1)} fusion(bf16[1024,12,64]{0,2,1:T(8,128)(2,1)S(1)} %bitcast.171, f32[12,512]{1,0:T(8,128)S(1)} %get-tuple-element.18, f32[12,512]{1,0:T(8,128)S(1)} %get-tuple-element.20, f32[12,512,1024]{2,1,0:T(8,128)} %fusion.66, pred[1024]{0:T(1024)(128)(4,1)S(1)} %broadcast_in_dim.138), kind=kOutput, calls=%fused_computation.87 | convolution fusion | flops 837156864 | bytes 27575296 | tf_op jit(solution)/shard_map/hqk,khd->qhd/dot_general | solution.py:73
  191.3 38.0 %all-gather.18.cloned.1.call-done = bf16[768,2048]{1,0:T(8,128)(2,1)} async-done(((bf16[48,2048]{1,0:T(8,128)(2,1)}), bf16[768,2048]{1,0:T(8,128)(2,1)}) %all-gather.18.cloned.1.call-update) | async-done | bytes 3145744 | tf_op jit(solution)/shard_map/all_gather | solution.py:191
  229.3 7.5 fusion.68
  236.8 38.5 %all-gather.16.cloned.1.call-done = bf16[768,2048]{1,0:T(8,128)(2,1)} async-done(((bf16[48,2048]{1,0:T(8,128)(2,1)}), bf16[768,2048]{1,0:T(8,128)(2,1)}) %all-gather.16.cloned.1.call-update) | async-done | bytes 3145744 | tf_op jit(solution)/shard_map/all_gather | solution.py:190
  275.3 9.0 %fusion.67 = f32[1024,2048]{1,0:T(8,128)} fusion(bf16[1024,768]{1,0:T(8,128)(2,1)} %copy-done.24, bf16[768,2048]{1,0:T(8,128)(2,1)} %all-gather.16.cloned.1.call-done), kind=kOutput, calls=%fused_computation.166 | convolution fusion | flops 3221225472 | bytes 13107200 | tf_op jit(solution)/shard_map/dot_general | solution.py:51
  284.3 37.1 %all-gather.20.cloned.1.call-done = bf16[2048,768]{1,0:T(8,128)(2,1)} async-done(((bf16[128,768]{1,0:T(8,128)(2,1)}), bf16[2048,768]{1,0:T(8,128)(2,1)}) %all-gather.20.cloned.1.call-update) | async-done | bytes 3145744 | tf_op jit(solution)/shard_map/all_gather | solution.py:192
  321.4 15.1 %multiply_convert_fusion.2 = (bf16[1024,2048]{1,0:T(8,128)(2,1)S(1)}, bf16[1024,2048]{1,0:T(8,128)(2,1)}, bf16[1024,2048]{1,0:T(8,128)(2,1)}) fusion(f32[1024,2048]{1,0:T(8,128)} %fusion.67, f32[1024,2048]{1,0:T(8,128)} %fusion.68, bf16[2048,768]{1,0:T(8,128)(2,1)} %all-gather.20.cloned.1.call-done, bf16[1,1,1024,768]{3,2,1,0:T(8,128)(2,1)S(1)} %copy-done.18, ...), kind=kOutput, calls=%fused_computation.36 | convolution fusion | flops 3278110720 | bytes 34079744 | tf_op jit(solution)/shard_map/dot_general | solution.py:45
  336.5 7.3 fusion.69
  343.8 4.6 multiply_reduce_fusion.2
  358.7 10.9 %fusion.70 = f32[12,512,1024]{2,1,0:T(8,128)} fusion(bf16[512,12,64]{0,2,1:T(8,128)(2,1)S(1)} %bitcast.176, bf16[1024,12,64]{0,2,1:T(8,128)(2,1)S(1)} %bitcast.172), kind=kOutput, calls=%fused_computation.169 | convolution fusion | flops 805306368 | bytes 27525120 | tf_op jit(solution)/shard_map/qhd,khd->hqk/dot_general | solution.py:99
  369.5 12.6 %fusion.4 = f32[12,64,1024]{2,1,0:T(8,128)} fusion(bf16[512,12,64]{0,2,1:T(8,128)(2,1)S(1)} %bitcast.177, f32[12,512]{1,0:T(8,128)S(1)} %get-tuple-element.68, f32[12,512,1024]{2,1,0:T(8,128)} %fusion.66, pred[1024]{0:T(1024)(128)(4,1)S(1)} %broadcast_in_dim.138), kind=kOutput, calls=%fused_computation.19 | convolution fusion | flops 830472192 | bytes 29123584 | tf_op jit(solution)/shard_map/hqk,qhd->khd/dot_general | solution.py:116
  382.1 35.6 %multiply_reduce_fusion.1 = (f32[12,512]{1,0:T(8,128)S(1)}, f32[12,512]{1,0:T(8,128)S(1)}, f32[12,512,1024]{2,1,0:T(8,128)}) fusion(f32[12,512]{1,0:T(8,128)S(1)} %get-tuple-element.69, f32[12,512,1024]{2,1,0:T(8,128)} %get-tuple-element.62, pred[1024]{0:T(1024)(128)(4,1)S(1)} %broadcast_in_dim.138, f32[12,512,1024]{2,1,0:T(8,128)} %fusion.70, ...), kind=kOutput, calls=%fused_computation.7 | convolution fusion | flops 868208640 | bytes 103121920 | tf_op jit(solution)/shard_map/qhd,khd->hqk/dot_general | solution.py:99
  417.7 12.3 %add_convert_fusion = bf16[12,64,1024]{2,1,0:T(8,128)(2,1)S(1)} fusion(f32[12,64,1024]{2,1,0:T(8,128)} %fusion.4, bf16[512,12,64]{0,2,1:T(8,128)(2,1)S(1)} %bitcast.182, f32[12,512]{1,0:T(8,128)S(1)} %get-tuple-element.69, f32[12,512,1024]{2,1,0:T(8,128)} %get-tuple-element.62, pred[1024]{0:T(1024)(128)(4,1)S(1)} %broadcast_in_dim.138), kind=kOutput, calls=%fused_computation.65 | convolution fusion | flops 832045056 | bytes 30696448 | tf_op jit(solution)/shard_map/hqk,qhd->khd/dot_general | solution.py:116
  433.7 42.7 %multiply_convert_fusion.1 = (bf16[12,512,1024]{2,1,0:T(8,128)(2,1)}, bf16[12,512,1024]{2,1,0:T(8,128)(2,1)}) fusion(f32[12,512,1024]{2,1,0:T(8,128)} %get-tuple-element.66, f32[12,512]{1,0:T(8,128)S(1)} %get-tuple-element.15, f32[12,512]{1,0:T(8,128)S(1)} %get-tuple-element.69, f32[12,512,1024]{2,1,0:T(8,128)} %get-tuple-element.62, ...), kind=kLoop, calls=%fused_computation.6 | loop fusion | flops 75497472 | bytes 125928448 | tf_op jit(solution)/shard_map/convert_element_type | solution.py:103
  476.3 8.6 multiply_convert_fusion.7
  484.9 8.7 multiply_convert_fusion.6
  496.4 6.9 fusion.71
  503.3 7.2 multiply_convert_fusion.4
  513.2 7.9 convolution_convert_fusion
  521.2 7.9 convolution_convert_fusion.2
  529.5 7.8 convolution_convert_fusion.1
  548.1 3.8 all-to-all-start
  553.5 60.5 %reduce-scatter.10.cloned.1.call-done = bf16[48,768]{1,0:T(8,128)(2,1)} async-done(((bf16[768,768]{1,0:T(8,128)(2,1)}), bf16[48,768]{1,0:T(8,128)(2,1)}) %reduce-scatter.10.cloned.1.call-update) | async-done | bytes 73744 | tf_op jit(solution)/shard_map/reduce_scatter | solution.py:269
  613.9 69.0 %reduce-scatter.20.cloned.1.call-done = bf16[128,768]{1,0:T(8,128)(2,1)} async-done(((bf16[2048,768]{1,0:T(8,128)(2,1)}), bf16[128,768]{1,0:T(8,128)(2,1)}) %reduce-scatter.20.cloned.1.call-update) | async-done | bytes 196624 | tf_op jit(solution)/shard_map/reduce_scatter | solution.py:225
  682.9 69.1 %reduce-scatter.16.cloned.1.call-done = bf16[48,2048]{1,0:T(8,128)(2,1)} async-done(((bf16[768,2048]{1,0:T(8,128)(2,1)}), bf16[48,2048]{1,0:T(8,128)(2,1)}) %reduce-scatter.16.cloned.1.call-update) | async-done | bytes 196624 | tf_op jit(solution)/shard_map/reduce_scatter | solution.py:219
  752.0 69.0 %reduce-scatter.18.cloned.1.call-done = bf16[48,2048]{1,0:T(8,128)(2,1)} async-done(((bf16[768,2048]{1,0:T(8,128)(2,1)}), bf16[48,2048]{1,0:T(8,128)(2,1)}) %reduce-scatter.18.cloned.1.call-update) | async-done | bytes 196624 | tf_op jit(solution)/shard_map/reduce_scatter | solution.py:222
  821.0 8.6 fusion.35
  829.6 29.5 %all-reduce.2 = (bf16[768]{0:T(1024)(128)(2,1)S(1)}, bf16[768]{0:T(1024)(128)(2,1)S(1)}) all-reduce(bf16[768]{0:T(1024)(128)(2,1)S(1)} %get-tuple-element.13, bf16[768]{0:T(1024)(128)(2,1)S(1)} %copy-done.38), channel_id=2, replica_groups=mesh['shard'=16,'replica'=2] {'shard'}, use_global_device_ids=true, to_apply=%region_16.17.clone | all-reduce | flops 1536 | bytes 6144
  859.3 4.9 all-reduce.3
  867.3 8.6 scatter_custom_fusion
  (221 shorter events, 85.0 us)
Async XLA Ops:
  7.2 7.8 copy-start
  7.2 98.4 %all-gather.10.cloned.1.call-start = ((), (), s32[]{:S(2)}) async-start(), calls=%async_computation.9 | async-start | bytes 1253376 | tf_op jit(solution)/shard_map/all_gather | solution.py:175
  7.9 101.0 %all-gather.12.cloned.1.call-start = ((), (), s32[]{:S(2)}) async-start(), calls=%async_computation.10 | async-start | bytes 1253376 | tf_op jit(solution)/shard_map/all_gather | solution.py:176
  8.7 150.1 %all-gather.8.cloned.1.call-start = ((), (), s32[]{:S(2)}) async-start(), calls=%async_computation.8 | async-start | bytes 1253376 | tf_op jit(solution)/shard_map/all_gather | solution.py:177
  9.4 176.6 %all-gather.14.cloned.1.call-start = ((), (), s32[]{:S(2)}) async-start(), calls=%async_computation.11 | async-start | bytes 1253376 | tf_op jit(solution)/shard_map/all_gather | solution.py:178
  10.0 219.3 %all-gather.18.cloned.1.call-start = ((), (), s32[]{:S(2)}) async-start(), calls=%async_computation.13 | async-start | bytes 3342336 | tf_op jit(solution)/shard_map/all_gather | solution.py:191
  10.6 264.7 %all-gather.16.cloned.1.call-start = ((), (), s32[]{:S(2)}) async-start(), calls=%async_computation.12 | async-start | bytes 3342336 | tf_op jit(solution)/shard_map/all_gather | solution.py:190
  11.2 310.2 %all-gather.20.cloned.1.call-start = ((), (), s32[]{:S(2)}) async-start(), calls=%async_computation.14 | async-start | bytes 3342336 | tf_op jit(solution)/shard_map/all_gather | solution.py:192
  20.6 78.1 %collective-permute-start.14 = (bf16[1,64,768]{2,1,0:T(8,128)(2,1)S(1)}, bf16[1,64,768]{2,1,0:T(8,128)(2,1)S(1)}, u32[]{:S(2)}, u32[]{:S(2)}) collective-permute-start(bf16[1,64,768]{2,1,0:T(8,128)(2,1)S(1)} %get-tuple-element.41), channel_id=1, source_target_pairs={{0,30},{2,28},{4,26},{6,24},{8,22},{10,20},{12,18},{14,16},{16,14}... | collective-permute-start | bytes 294920 | tf_op jit(solution)/shard_map/ppermute | solution.py:167
  26.1 72.6 %collective-permute-start.13 = (bf16[1,64,768]{2,1,0:T(8,128)(2,1)S(1)}, bf16[1,64,768]{2,1,0:T(8,128)(2,1)S(1)}, u32[]{:S(2)}, u32[]{:S(2)}) collective-permute-start(bf16[1,64,768]{2,1,0:T(8,128)(2,1)S(1)} %get-tuple-element.42), channel_id=1, source_target_pairs={{0,28},{2,30},{4,24},{6,26},{8,20},{10,22},{12,16},{14,18},{16,12}... | collective-permute-start | bytes 294920 | tf_op jit(solution)/shard_map/ppermute | solution.py:167
  26.7 71.9 %collective-permute-start.12 = (bf16[1,64,768]{2,1,0:T(8,128)(2,1)S(1)}, bf16[1,64,768]{2,1,0:T(8,128)(2,1)S(1)}, u32[]{:S(2)}, u32[]{:S(2)}) collective-permute-start(bf16[1,64,768]{2,1,0:T(8,128)(2,1)S(1)} %get-tuple-element.43), channel_id=1, source_target_pairs={{0,26},{2,24},{4,30},{6,28},{8,18},{10,16},{12,22},{14,20},{16,10}... | collective-permute-start | bytes 294920 | tf_op jit(solution)/shard_map/ppermute | solution.py:167
  29.9 68.7 %collective-permute-start.11 = (bf16[1,64,768]{2,1,0:T(8,128)(2,1)S(1)}, bf16[1,64,768]{2,1,0:T(8,128)(2,1)S(1)}, u32[]{:S(2)}, u32[]{:S(2)}) collective-permute-start(bf16[1,64,768]{2,1,0:T(8,128)(2,1)S(1)} %get-tuple-element.44), channel_id=1, source_target_pairs={{0,24},{2,26},{4,28},{6,30},{8,16},{10,18},{12,20},{14,22},{16,8},... | collective-permute-start | bytes 294920 | tf_op jit(solution)/shard_map/ppermute | solution.py:167
  30.2 1.9 collective-permute-start
  30.4 523.0 %reduce-scatter.14.cloned.1.call-start = ((), (), s32[]{:S(2)}) async-start(), calls=%async_computation.18 | async-start | bytes 1253376 | tf_op jit(solution)/shard_map/reduce_scatter | solution.py:275
  32.2 5.1 collective-permute-start.1
  37.3 5.0 collective-permute-start.2
  42.3 4.8 collective-permute-start.3
  47.1 5.2 collective-permute-start.4
  52.3 6.5 collective-permute-start.5
  58.8 5.2 collective-permute-start.6
  64.0 8.6 collective-permute-start.7
  72.6 29.9 %copy-start.28 = (f32[768]{0:T(1024)S(1)}, f32[768]{0:T(1024)}, u32[]{:S(2)}) copy-start(f32[768]{0:T(1024)} %param.16) | copy-start | bytes 9220
  72.6 9.2 %collective-permute-start.8 = (bf16[1,64,768]{2,1,0:T(8,128)(2,1)S(1)}, bf16[1,64,768]{2,1,0:T(8,128)(2,1)S(1)}, u32[]{:S(2)}, u32[]{:S(2)}) collective-permute-start(bf16[1,64,768]{2,1,0:T(8,128)(2,1)S(1)} %get-tuple-element.47), channel_id=1, source_target_pairs={{0,18},{2,16},{4,22},{6,20},{8,26},{10,24},{12,30},{14,28},{16,2},... | collective-permute-start | bytes 294920 | tf_op jit(solution)/shard_map/ppermute | solution.py:167
  81.7 6.7 collective-permute-start.9
  88.5 10.2 %collective-permute-start.10 = (bf16[1,64,768]{2,1,0:T(8,128)(2,1)S(1)}, bf16[1,64,768]{2,1,0:T(8,128)(2,1)S(1)}, u32[]{:S(2)}, u32[]{:S(2)}) collective-permute-start(bf16[1,64,768]{2,1,0:T(8,128)(2,1)S(1)} %get-tuple-element.45), channel_id=1, source_target_pairs={{0,22},{2,20},{4,18},{6,16},{8,30},{10,28},{12,26},{14,24},{16,6},... | collective-permute-start | bytes 294920 | tf_op jit(solution)/shard_map/ppermute | solution.py:167
  102.0 84.0 %copy-start.2 = (bf16[16,64,768]{2,1,0:T(8,128)(2,1)}, bf16[16,64,768]{2,1,0:T(8,128)(2,1)S(1)}, u32[]{:S(2)}) copy-start(bf16[16,64,768]{2,1,0:T(8,128)(2,1)S(1)} %gather_fusion.1) | copy-start | bytes 4718596
  108.9 14.5 %copy-start.14 = (bf16[512,768]{0,1:T(8,128)(2,1)}, bf16[512,768]{0,1:T(8,128)(2,1)S(1)}, u32[]{:S(2)}) copy-start(bf16[512,768]{0,1:T(8,128)(2,1)S(1)} %get-tuple-element.40) | copy-start | bytes 2359300
  112.7 10.7 %copy-start.4 = (bf16[1024,768]{0,1:T(8,128)(2,1)}, bf16[1024,768]{0,1:T(8,128)(2,1)S(1)}, u32[]{:S(2)}) copy-start(bf16[1024,768]{0,1:T(8,128)(2,1)S(1)} %convolution_convert_fusion.4) | copy-start | bytes 4718596
  162.0 11.7 %copy-start.8 = (bf16[1024,768]{0,1:T(8,128)(2,1)}, bf16[1024,768]{0,1:T(8,128)(2,1)S(1)}, u32[]{:S(2)}) copy-start(bf16[1024,768]{0,1:T(8,128)(2,1)S(1)} %convolution_convert_fusion.6) | copy-start | bytes 4718596
  191.3 38.0 %copy-start.24 = (bf16[1024,768]{1,0:T(8,128)(2,1)}, bf16[1024,768]{1,0:T(8,128)(2,1)S(1)}, u32[]{:S(2)}) copy-start(bf16[1024,768]{1,0:T(8,128)(2,1)S(1)} %multiply_convert_fusion.5) | copy-start | bytes 4718596
  236.8 84.6 %copy-start.18 = (bf16[1,1,1024,768]{3,2,1,0:T(8,128)(2,1)S(1)}, bf16[1,1,1024,768]{3,2,1,0:T(8,128)(2,1)}, u32[]{:S(2)}) copy-start(bf16[1,1,1024,768]{3,2,1,0:T(8,128)(2,1)} %param.25) | copy-start | bytes 4718596
  321.4 15.1 %copy-start.40 = (bf16[768,2048]{1,0:T(8,128)(2,1)S(1)}, bf16[768,2048]{1,0:T(8,128)(2,1)}, u32[]{:S(2)}) copy-start(bf16[768,2048]{1,0:T(8,128)(2,1)} %all-gather.16.cloned.1.call-done) | copy-start | bytes 9437188
  336.5 7.3 copy-start.13
  336.5 7.3 copy-start.39
  353.9 199.6 %reduce-scatter.12.cloned.1.call-start = ((), (), s32[]{:S(2)}) async-start(), calls=%async_computation.17 | async-start | bytes 1253376 | tf_op jit(solution)/shard_map/reduce_scatter | solution.py:272
  417.7 13.4 %copy-start.21 = (bf16[16,1,64,768]{3,2,0,1:T(8,128)(2,1)S(1)}, bf16[16,1,64,768]{3,2,0,1:T(8,128)(2,1)}, u32[]{:S(2)}) copy-start(bf16[16,1,64,768]{3,2,0,1:T(8,128)(2,1)} %fusion.27) | copy-start | bytes 4718596
  433.6 119.8 %reduce-scatter.8.cloned.1.call-start = ((), (), s32[]{:S(2)}) async-start(), calls=%async_computation.15 | async-start | bytes 1253376 | tf_op jit(solution)/shard_map/reduce_scatter | solution.py:266
  433.7 42.7 %copy-start.5 = (bf16[1024,768]{0,1:T(8,128)(2,1)S(1)}, bf16[1024,768]{0,1:T(8,128)(2,1)}, u32[]{:S(2)}) copy-start(bf16[1024,768]{0,1:T(8,128)(2,1)} %copy-done.4) | copy-start | bytes 4718596
  484.9 8.7 copy-start.23
  496.1 117.8 %reduce-scatter.10.cloned.1.call-start = ((), (), s32[]{:S(2)}) async-start(), calls=%async_computation.16 | async-start | bytes 1253376 | tf_op jit(solution)/shard_map/reduce_scatter | solution.py:269
  513.1 169.8 %reduce-scatter.20.cloned.1.call-start = ((), (), s32[]{:S(2)}) async-start(), calls=%async_computation.21 | async-start | bytes 3342336 | tf_op jit(solution)/shard_map/reduce_scatter | solution.py:225
  521.1 230.9 %reduce-scatter.16.cloned.1.call-start = ((), (), s32[]{:S(2)}) async-start(), calls=%async_computation.19 | async-start | bytes 3342336 | tf_op jit(solution)/shard_map/reduce_scatter | solution.py:219
  529.1 291.9 %reduce-scatter.18.cloned.1.call-start = ((), (), s32[]{:S(2)}) async-start(), calls=%async_computation.20 | async-start | bytes 3342336 | tf_op jit(solution)/shard_map/reduce_scatter | solution.py:222
  548.1 317.2 %all-to-all-start = ((bf16[16,64,768]{2,1,0:T(8,128)(2,1)}), bf16[16,64,768]{2,1,0:T(8,128)(2,1)S(1)}, u32[]{:S(2)}, u32[]{:S(2)}) async-start(bf16[16,64,768]{2,1,0:T(8,128)(2,1)} %bitcast.45), calls=%async_computation | async-start | bytes 3145728 | tf_op jit(solution)/shard_map/all_to_all | solution.py:258
  551.9 324.9 %all-reduce.7.cloned.1.call-start = ((), (), s32[]{:S(2)}) async-start(), calls=%async_computation.22 | async-start | bytes 1769472 | tf_op jit(solution)/shard_map/psum | solution.py:287
  821.0 8.6 copy-start.38
  821.0 44.2 %copy-start.35 = (pred[16,64]{1,0:T(8,128)(4,1)S(1)}, pred[16,64]{1,0:T(8,128)(4,1)}, u32[]{:S(2)}) copy-start(pred[16,64]{1,0:T(8,128)(4,1)} %copy-done.34) | copy-start | bytes 3076
  867.3 20.9 %copy-start.1 = (bf16[1,512,768]{2,1,0:T(8,128)(2,1)S(1)}, bf16[1,512,768]{2,1,0:T(8,128)(2,1)}, u32[]{:S(2)}) copy-start(bf16[1,512,768]{2,1,0:T(8,128)(2,1)} %param.13) | copy-start | bytes 2359300
  (29 other events, 81.2 us)
Sparse Core Ops, SparseCore 0:
  10.3 50.2 all-gather.9
  62.9 40.9 all-gather.11
  106.1 37.2 all-gather.7
  145.5 37.1 all-gather.13
  184.9 44.3 all-gather.17
  231.4 43.8 all-gather.15
  277.5 43.8 all-gather.19
  354.0 56.4 reduce-scatter.13
  433.7 56.5 reduce-scatter.11
  496.2 56.5 reduce-scatter.7
  556.5 57.4 reduce-scatter.9
  617.6 65.2 reduce-scatter.19
  686.7 65.2 reduce-scatter.15
  755.7 65.2 reduce-scatter.17
  823.5 35.5 all-reduce.6
